TPU v7x, 256 devices: a whole 4x4x8 slice. The times are simulated.
256 devices in a mesh: img: 64 (over x, z, y_lo), txt: 4 (over y_hi, core).
Axes of the slice: x: 4, y: 4 (y_hi: 2, y_lo: 2; y = y_hi * 2 + y_lo), z: 8, core: 2. Of those that a mesh axis runs over, the one named last changes fastest.
Arguments:
- image_tokens: bfloat16 [32768, 256], P(('img', 'txt')), may hold values from -6 to 6
- prompt_tokens: bfloat16 [6144, 256], P(('txt', 'img')), may hold values from -6 to 6
- category_ids: int32 [6144], P(('txt', 'img')), may hold values from 0 to 383, as said below
- prompt_valid: int32 [6144], P(('txt', 'img')), may hold values from 0 to 1, as said below
- image_gain: float32 [256], replicated, may hold values from 0.5 to 1.5
- prompt_gain: float32 [256], replicated, may hold values from 0.5 to 1.5
- query_weight: bfloat16 [256, 1024], replicated, may hold values from -1.7 to 1.7
- key_weight: bfloat16 [256, 1024], replicated, may hold values from -1.7 to 1.7
- image_value_weight: bfloat16 [256, 1024], replicated, may hold values from -0.375 to 0.375
- prompt_value_weight: bfloat16 [256, 1024], replicated, may hold values from -0.375 to 0.375
- image_out_weight: bfloat16 [1024, 256], replicated, may hold values from -0.1875 to 0.1875
- prompt_out_weight: bfloat16 [1024, 256], replicated, may hold values from -0.1875 to 0.1875
- image_layer_scale: float32 [256], replicated, may hold values from 1 to 4
- prompt_layer_scale: float32 [256], replicated, may hold values from 1 to 4
Outputs:
- joined_image: bfloat16 [32768, 256], P(('img', 'txt'))
- joined_prompt: bfloat16 [6144, 256], P(('txt', 'img'))
- category_embed: float32 [384, 256], replicated
Inputs may be any that keep to these rules, and one draw needn't show every extreme that they name: `category_ids`: along the prompt the ids never fall; each of the 384 categories holds between 4 and 28 consecutive tokens. `prompt_valid`: within each category the tokens marked 1 come first, and at least one token is marked 1.
All inputs are finite; a program needn't handle non-finite values.
Results may differ from a plain program's by a relative error of at most 0.009.
The roundings to bfloat16 on the way count: a program that leaves them out, or rounds other values in their place, can miss the bound.
Values may be sent and summed in bfloat16 or wider, within the bound.
No kernel may reach another device: no remote copies, remote signals or barrier semaphores. Data moves between devices by JAX's collectives and lax.ppermute only.
A program may use at most 128 MiB of HBM per device.

v0:
```python
import math
import jax
import jax.numpy as jnp
from jax import lax
from jax.sharding import Mesh
from jax.sharding import PartitionSpec as P

HD = 256
IMG = ("img_0", "img_1", "img_2")
IMG_TXT = ("img_0", "img_1", "img_2", "txt")
TXT_IMG = ("txt", "img_0", "img_1", "img_2")
EPSILON = 1e-05
MASKED = -1e30


def sent_to_all(shard, axis):
    copies = jnp.broadcast_to(shard, (lax.axis_size(axis), *shard.shape))
    return lax.all_to_all(copies, axis, split_axis=0, concat_axis=0, tiled=True)


def in_order(parts, dim):
    parts = jnp.moveaxis(parts, 0, dim)
    lengths = parts.shape
    return parts.reshape(*lengths[:dim], lengths[dim] * lengths[dim + 1], *lengths[dim + 2 :])


def gather_directly(shard, axis, dim):
    parts = sent_to_all(shard, axis)
    return in_order(parts, dim)


def in_one_piece(arrays, axis, dim, along):
    columns = [a.reshape(*a.shape[:along], -1) for a in arrays]
    both = jnp.concatenate(columns, axis=along)
    filled, at, done = (lax.all_gather(both, axis, axis=dim, tiled=True), 0, [])
    for a, column in zip(arrays, columns):
        piece = filled[..., at : at + column.shape[along]]
        done.append(piece.reshape(*piece.shape[:along], *a.shape[along:]))
        at += column.shape[along]
    return tuple(done)


def collected_together(shard, axis):
    leaves = jax.tree.leaves(shard)
    sequence = sorted(range(len(leaves)), key=lambda k: -leaves[k].size)
    width = (1, *leaves[sequence[0]].shape)[-1]
    lines = [
        jnp.pad(leaves[k].reshape(-1), (0, -leaves[k].size % width)).reshape(-1, width)
        for k in sequence
    ]
    both, at, found = (sent_to_all(jnp.concatenate(lines), axis), 0, {})
    for k, line in zip(sequence, lines):
        piece = both[:, at : at + len(line)].reshape(len(both), -1)
        found[k] = piece[:, : leaves[k].size].reshape(-1, *leaves[k].shape)
        at += len(line)
    numbers = iter(range(len(leaves)))
    return jax.tree.map(lambda _: found[next(numbers)], shard)


def joined_by_halves(pieces, combine):
    while len(jax.tree.leaves(pieces)[0]) > 1:
        pieces = jax.vmap(combine)(
            *(jax.tree.map(lambda part: part[side::2], pieces) for side in (0, 1))
        )
    return jax.tree.map(lambda part: part[0], pieces)


def joined_all(shard, axis, combine):
    pieces = collected_together(shard, axis)
    return joined_by_halves(pieces, combine)


def collected_together_2(shard, axis):
    leaves = jax.tree.leaves(shard)
    sequence = sorted(range(len(leaves)), key=lambda k: -leaves[k].size)
    width = (1, *leaves[sequence[0]].shape)[-1]
    lines = [
        jnp.pad(leaves[k].reshape(-1), (0, -leaves[k].size % width)).reshape(-1, width)
        for k in sequence
    ]
    both, at, found = (lax.all_gather(jnp.concatenate(lines), axis), 0, {})
    for k, line in zip(sequence, lines):
        piece = both[:, at : at + len(line)].reshape(len(both), -1)
        found[k] = piece[:, : leaves[k].size].reshape(-1, *leaves[k].shape)
        at += len(line)
    numbers = iter(range(len(leaves)))
    return jax.tree.map(lambda _: found[next(numbers)], shard)


def joined_all_2(shard, axes, combine):
    for axis in axes:
        pieces = collected_together_2(shard, axis)
        shard = jax.tree.map(lambda part: part[0], pieces)
        for k in range(1, lax.axis_size(axis)):
            shard = combine(shard, jax.tree.map(lambda part: part[k], pieces))
    return shard


def cut_along(shard, dim, size):
    lengths = shard.shape
    parts = shard.reshape(*lengths[:dim], size, lengths[dim] // size, *lengths[dim + 1 :])
    return jnp.moveaxis(parts, dim, 0)


def sent_and_summed(shard, axis, dim):
    size = lax.axis_size(axis)
    parts = lax.all_to_all(cut_along(shard, dim, size), axis, 0, 0, tiled=True)
    return jnp.sum(parts.astype(jnp.float32), axis=0)


def sent_and_summed_2(shard, axis, dim):
    parts = cut_along(shard, dim, lax.axis_size(axis))
    arrived = lax.all_to_all(parts, axis, split_axis=0, concat_axis=0, tiled=True)
    return arrived.sum(axis=0)


def together(arrays, axis):
    ravelled, at, done = (jnp.concatenate([a.reshape(-1) for a in arrays]), 0, [])
    total = lax.psum(ravelled, axis)
    for a in arrays:
        done.append(total[at : at + a.size].reshape(a.shape))
        at += a.size
    return tuple(done)


def normalize(tokens_in, gain_row):
    values = tokens_in.astype(jnp.float32)
    average = jnp.mean(values, axis=-1, keepdims=True)
    centered = values - average
    variance = jnp.mean(centered * centered, axis=-1, keepdims=True)
    return (centered * lax.rsqrt(variance + EPSILON) * gain_row).astype(jnp.bfloat16)


def combine_stats(left_stats, right_stats):
    highest = jnp.maximum(left_stats[0], right_stats[0])
    summed = left_stats[1] * jnp.exp(left_stats[0] - highest) + right_stats[1] * jnp.exp(
        right_stats[0] - highest
    )
    return (highest, summed)


def on_device(
    image_tokens,
    prompt_tokens,
    category_ids,
    prompt_valid,
    image_gain,
    prompt_gain,
    query_weight,
    key_weight,
    image_value_weight,
    prompt_value_weight,
    image_out_weight,
    prompt_out_weight,
    image_layer_scale,
    prompt_layer_scale,
):
    embed_width = query_weight.shape[1]
    head_count = embed_width // HD
    image_normed = normalize(image_tokens, image_gain)
    image_weights = jnp.concatenate([query_weight, image_value_weight], axis=1)
    image_projected = jnp.dot(
        gather_directly(image_normed, "txt", 0), image_weights, preferred_element_type=jnp.float32
    ).astype(jnp.bfloat16)
    prompt_normed = normalize(prompt_tokens, prompt_gain)
    prompt_weights = jnp.concatenate([key_weight, prompt_value_weight], axis=1)
    valid_marks = prompt_valid.astype(jnp.bfloat16)
    gathered, marks_all = in_one_piece((prompt_normed, valid_marks), IMG, 0, 1)
    prompt_projected = jnp.dot(gathered, prompt_weights, preferred_element_type=jnp.float32).astype(
        jnp.bfloat16
    )
    image_count = image_projected.shape[0]
    prompt_count = prompt_projected.shape[0]
    query_heads = image_projected[:, :embed_width].reshape(image_count, head_count, HD)
    image_value_heads = image_projected[:, embed_width:].reshape(image_count, head_count, HD)
    key_heads = prompt_projected[:, :embed_width].reshape(prompt_count, head_count, HD)
    prompt_value_heads = prompt_projected[:, embed_width:].reshape(prompt_count, head_count, HD)
    scores = jnp.einsum(
        "ihd,thd->hit", query_heads, key_heads, preferred_element_type=jnp.float32
    ) / math.sqrt(HD)
    is_valid = (marks_all > 0)[None, None, :]
    masked = jnp.where(is_valid, scores, MASKED)
    local_row_top = jnp.max(masked, axis=2)
    local_row_sum = jnp.sum(
        jnp.where(is_valid, jnp.exp(masked - local_row_top[:, :, None]), 0.0), axis=2
    )
    row_top, row_sum = joined_all((local_row_top, local_row_sum), "txt", combine_stats)
    local_col_top = jnp.max(scores, axis=1)
    local_col_sum = jnp.sum(jnp.exp(scores - local_col_top[:, None, :]), axis=1)
    col_top, col_sum = joined_all_2((local_col_top, local_col_sum), IMG, combine_stats)
    row_weights = jnp.where(is_valid, jnp.exp(masked - row_top[:, :, None]), 0.0).astype(
        jnp.bfloat16
    )
    col_weights = jnp.exp(scores - col_top[:, None, :]).astype(jnp.bfloat16)
    image_numer = jnp.einsum(
        "hit,thd->ihd", row_weights, prompt_value_heads, preferred_element_type=jnp.float32
    )
    image_part = (
        (image_numer / row_sum.T[:, :, None]).reshape(image_count, embed_width).astype(jnp.bfloat16)
    )
    block_rows = image_part
    image_delta = sent_and_summed(
        jnp.dot(block_rows, image_out_weight, preferred_element_type=jnp.float32).astype(
            jnp.bfloat16
        ),
        "txt",
        0,
    )
    joined_image = (image_tokens.astype(jnp.float32) + image_layer_scale * image_delta).astype(
        jnp.bfloat16
    )
    prompt_numer = jnp.einsum(
        "hit,ihd->thd", col_weights, image_value_heads, preferred_element_type=jnp.float32
    )
    prompt_part = (
        (prompt_numer / col_sum.T[:, :, None])
        .reshape(prompt_count, embed_width)
        .astype(jnp.bfloat16)
    )
    block_rows = prompt_part
    prompt_delta = sent_and_summed_2(
        jnp.dot(block_rows, prompt_out_weight, preferred_element_type=jnp.float32), IMG, 0
    )
    prompt_joined = prompt_tokens.astype(jnp.float32) + prompt_layer_scale * prompt_delta
    category_count = prompt_count * lax.axis_size("txt") // 16
    members = jnp.logical_and(
        category_ids[None, :] == jnp.arange(category_count, dtype=jnp.int32)[:, None],
        prompt_valid[None, :] > 0,
    ).astype(jnp.float32)
    category_sum = jnp.dot(members, prompt_joined)
    category_tally = jnp.sum(members, axis=1)
    category_sum, category_tally = together((category_sum, category_tally), IMG_TXT)
    category_embed = category_sum / category_tally[:, None]
    return (joined_image, prompt_joined.astype(jnp.bfloat16), category_embed)


def solution(mesh):
    finer = Mesh(
        mesh.devices.reshape(4, 8, 2, mesh.shape["txt"]), ("img_0", "img_1", "img_2", "txt")
    )
    return jax.shard_map(
        on_device,
        mesh=finer,
        in_specs=(
            P(IMG_TXT, None),
            P(TXT_IMG, None),
            P(TXT_IMG),
            P(TXT_IMG),
            P(),
            P(),
            P(),
            P(),
            P(),
            P(),
            P(),
            P(),
            P(),
            P(),
        ),
        out_specs=(P(IMG_TXT, None), P(TXT_IMG, None), P()),
        check_vma=False,
    )
```

profile of v0, /device:TPU:1, one launch (start us, length us, event | category | flops | bytes accessed | tf_op | source)
XLA Modules:
  0.0 599.6 jit_solution(7328133230477263510)
XLA Ops:
  7.2 0.0 copy-start
  7.2 1.0 convert_reduce_fusion.1
  8.2 1.0 fusion.23
  9.2 1.0 fusion.25
  10.2 0.7 broadcast_in_dim.27
  10.9 6.6 %all-to-all-start = ((bf16[4,128,256]{2,1,0:T(8,128)(2,1)}), bf16[4,128,256]{2,1,0:T(8,128)(2,1)S(1)}, u32[]{:S(2)}, u32[]{:S(2)}) async-start(bf16[4,128,256]{2,1,0:T(8,128)(2,1)} %broadcast_in_dim.27), calls=%async_computation | async-start | bytes 524288 | tf_op jit(solution)/shard_map/all_to_all | solution.py:18
  17.5 0.7 convert_bitcast_fusion
  18.1 0.1 copy.29
  18.2 0.8 convert_reduce_fusion.2
  19.1 0.9 fusion.31
  20.0 0.8 fusion.33
  20.8 136.4 %all_gather.21 = bf16[1536,257]{1,0:T(8,128)(2,1)S(1)} all-gather(bf16[24,257]{1,0:T(8,128)(2,1)S(1)} %pad_maximum_fusion.4), channel_id=1, replica_groups=mesh['img_0'=4,'img_1'=8,'img_2'=2,'txt'=4] {'img_0','img_1','img_2'}, dimensions={0}, use_global_device_ids=true | all-gather | bytes 801840 | tf_op jit(solution)/shard_map/all_gather | solution.py:35
  157.2 3.0 convolution_convert_fusion
  160.2 3.5 fusion.94
  163.8 4.8 copy.35
  168.6 0.3 compare_reduce_fusion
  168.8 0.0 all-to-all-done
  168.9 0.0 copy-start.2
  168.9 0.0 copy-done.4
  168.9 0.7 convolution_convert_fusion.1
  169.6 0.2 fusion.95
  169.8 1.0 copy-done.2
  170.7 2.5 multiply_reduce_fusion
  173.3 5.3 exponential_reduce_fusion
  178.6 0.6 broadcast_in_dim.50
  179.3 32.9 %all-to-all-start.1 = ((f32[4,8,512]{2,1,0:T(8,128)}), f32[4,8,512]{2,1,0:T(8,128)S(1)}, u32[]{:S(2)}, u32[]{:S(2)}) async-start(f32[4,8,512]{2,1,0:T(8,128)} %broadcast_in_dim.50), calls=%async_computation.1 | async-start | bytes 131072 | tf_op jit(solution)/shard_map/all_to_all | solution.py:18
  212.1 9.5 %all-gather = f32[32,1536]{1,0:T(8,128)S(1)} all-gather(f32[8,1536]{1,0:T(8,128)S(1)} %pad_maximum_fusion.1), channel_id=2, replica_groups=mesh['img_0'=4,'img_1'=8,'img_2'=2,'txt'=4] {'img_0'}, dimensions={0}, use_global_device_ids=true | all-gather | bytes 245760 | tf_op jit(solution)/shard_map/all_gather | solution.py:81
  221.7 0.1 fusion.60
  221.8 19.3 %all-gather.1 = f32[64,1536]{1,0:T(8,128)S(1)} all-gather(f32[8,1536]{1,0:T(8,128)S(1)} %pad_maximum_fusion.2), channel_id=3, replica_groups=mesh['img_0'=4,'img_1'=8,'img_2'=2,'txt'=4] {'img_1'}, dimensions={0}, use_global_device_ids=true | all-gather | bytes 442368 | tf_op jit(solution)/shard_map/all_gather | solution.py:81
  241.1 0.1 fusion.39
  241.3 3.8 all-gather.2
  245.1 0.5 copy.36
  245.7 9.1 %fusion.1 = bf16[1536,4,256]{0,2,1:T(8,128)(2,1)} fusion(f32[1536,4]{0,1:T(4,128)S(1)} %get-tuple-element.7, bf16[512,4,256]{0,2,1:T(8,128)(2,1)S(1)} %bitcast.311, f32[4,512,1536]{2,1,0:T(8,128)} %copy-done.1, f32[4,1536]{1,0:T(4,128)S(1)} %get-tuple-element.8), kind=kOutput, calls=%fused_computation.9 | convolution fusion | flops 1623195648 | bytes 16826368 | tf_op jit(solution)/shard_map/hit,ihd->thd/dot_general | solution.py:212
  254.7 5.9 copy.34
  260.6 6.1 %convert_element_type.72 = bf16[64,24,1024]{2,1,0:T(8,128)(2,1)} reshape(bf16[1536,4,256]{2,1,0:T(4,128)(2,1)} %copy.34) | data formatting | bytes 6291456 | tf_op jit(solution)/shard_map/convert_element_type | solution.py:218
  266.7 0.0 all-to-all-done.1
  266.8 0.0 copy-start.10
  266.8 8.7 %fusion.9 = bf16[512,4,256]{0,2,1:T(8,128)(2,1)S(1)} fusion(bf16[1536,4,256]{0,2,1:T(8,128)(2,1)} %bitcast.306, f32[4,512,1536]{2,1,0:T(8,128)} %copy-done.1, f32[4,512]{1,0:T(4,128)S(1)} %get-tuple-element.22, pred[1536]{0:T(1024)(128)(4,1)S(1)} %compare_reduce_fusion, f32[512,4]{0,1:T(4,128)S(1)} %get-tuple-element.21), kind=kOutput, calls=%fused_computation.19 | convolution fusion | flops 1627389952 | bytes 16795136 | tf_op jit(solution)/shard_map/hit,thd->ihd/dot_general | solution.py:195
  275.5 0.0 copy-start.11
  275.5 0.0 copy-start.8
  275.5 0.0 copy-start.3
  275.6 0.0 copy-start.9
  275.6 0.0 copy-start.6
  275.6 0.0 copy-start.7
  275.6 1.2 convolution_convert_fusion.2
  276.8 14.4 %all-to-all-start.2 = ((bf16[4,128,256]{2,1,0:T(8,128)(2,1)}), bf16[4,128,256]{2,1,0:T(8,128)(2,1)S(1)}, u32[]{:S(2)}, u32[]{:S(2)}) async-start(bf16[4,128,256]{2,1,0:T(8,128)(2,1)} %bitcast.8), calls=%async_computation.2 | async-start | bytes 524288 | tf_op jit(solution)/shard_map/all_to_all | solution.py:107
  291.2 4.0 fusion.19
  295.2 2.5 all-to-all-done.2
  297.7 4.7 all-to-all-start.3
  302.4 0.0 all-reduce.2.cloned.1.call-start
  302.5 0.1 convert_reduce_fusion.3
  302.6 0.7 fusion.26
  303.3 37.4 %all-to-all-done.3 = f32[64,24,256]{2,1,0:T(8,128)S(1)} async-done(((f32[64,24,256]{2,1,0:T(8,128)}), f32[64,24,256]{2,1,0:T(8,128)S(1)}, u32[]{:S(2)}, u32[]{:S(2)}) %all-to-all-start.3) | async-done | bytes 1572896 | tf_op jit(solution)/shard_map/all_to_all | solution.py:113
  340.7 0.1 reduce_sum.88
  340.9 0.3 convolution_bitcast_fusion
  341.2 0.2 copy.39
  341.4 0.8 pad_maximum_fusion
  342.2 0.0 all-reduce.2.cloned.1.call-update
  342.2 0.6 fusion.81
  342.8 247.2 %all-reduce.2.cloned.1.call-done = f32[98688]{0:T(1024)} async-done(((f32[98688]{0:T(1024)}), f32[98688]{0:T(1024)}) %all-reduce.2.cloned.1.call-update) | async-done | bytes 394768 | tf_op jit(solution)/shard_map/psum | solution.py:119
  590.1 1.0 slice.262
  591.1 0.1 reshape.118
  591.2 0.7 slice.263
  591.9 0.9 broadcast_divide_fusion
  (28 shorter events, 0.2 us)
Async XLA Ops:
  7.2 284.0 %copy-start = (bf16[1024,256]{1,0:T(8,128)(2,1)S(1)}, bf16[1024,256]{1,0:T(8,128)(2,1)}, u32[]{:S(2)}) copy-start(bf16[1024,256]{1,0:T(8,128)(2,1)} %param.25) | copy-start | bytes 1572868
  10.9 157.9 %all-to-all-start = ((bf16[4,128,256]{2,1,0:T(8,128)(2,1)}), bf16[4,128,256]{2,1,0:T(8,128)(2,1)S(1)}, u32[]{:S(2)}, u32[]{:S(2)}) async-start(bf16[4,128,256]{2,1,0:T(8,128)(2,1)} %broadcast_in_dim.27), calls=%async_computation | async-start | bytes 524288 | tf_op jit(solution)/shard_map/all_to_all | solution.py:18
  163.8 5.1 copy-start.4
  163.8 5.1 copy-start.5
  168.9 1.9 copy-start.2
  173.3 5.3 copy-start.1
  179.3 87.5 %all-to-all-start.1 = ((f32[4,8,512]{2,1,0:T(8,128)}), f32[4,8,512]{2,1,0:T(8,128)S(1)}, u32[]{:S(2)}, u32[]{:S(2)}) async-start(f32[4,8,512]{2,1,0:T(8,128)} %broadcast_in_dim.50), calls=%async_computation.1 | async-start | bytes 131072 | tf_op jit(solution)/shard_map/all_to_all | solution.py:18
  266.8 8.8 %copy-start.10 = (bf16[1024,256]{1,0:T(8,128)(2,1)S(1)}, bf16[1024,256]{1,0:T(8,128)(2,1)}, u32[]{:S(2)}) copy-start(bf16[1024,256]{1,0:T(8,128)(2,1)} %param.24) | copy-start | bytes 1572868
  275.5 26.9 %copy-start.11 = (s32[24]{0:T(128)S(1)}, s32[24]{0:T(128)}, u32[]{:S(2)}) copy-start(s32[24]{0:T(128)} %param.17) | copy-start | bytes 292
  275.5 27.0 %copy-start.8 = (s32[24]{0:T(128)S(1)}, s32[24]{0:T(128)}, u32[]{:S(2)}) copy-start(s32[24]{0:T(128)} %param.16) | copy-start | bytes 292
  275.5 27.1 %copy-start.3 = (bf16[128,256]{1,0:T(8,128)(2,1)S(1)}, bf16[128,256]{1,0:T(8,128)(2,1)}, u32[]{:S(2)}) copy-start(bf16[128,256]{1,0:T(8,128)(2,1)} %param.14) | copy-start | bytes 196612
  275.6 27.1 %copy-start.9 = (f32[256]{0:T(256)S(1)}, f32[256]{0:T(256)}, u32[]{:S(2)}) copy-start(f32[256]{0:T(256)} %param.26) | copy-start | bytes 3076
  275.6 65.3 %copy-start.6 = (bf16[24,256]{1,0:T(8,128)(2,1)S(1)}, bf16[24,256]{1,0:T(8,128)(2,1)}, u32[]{:S(2)}) copy-start(bf16[24,256]{1,0:T(8,128)(2,1)} %param.15) | copy-start | bytes 36868
  275.6 65.3 %copy-start.7 = (f32[256]{0:T(256)S(1)}, f32[256]{0:T(256)}, u32[]{:S(2)}) copy-start(f32[256]{0:T(256)} %param.27) | copy-start | bytes 3076
  276.8 20.9 %all-to-all-start.2 = ((bf16[4,128,256]{2,1,0:T(8,128)(2,1)}), bf16[4,128,256]{2,1,0:T(8,128)(2,1)S(1)}, u32[]{:S(2)}, u32[]{:S(2)}) async-start(bf16[4,128,256]{2,1,0:T(8,128)(2,1)} %bitcast.8), calls=%async_computation.2 | async-start | bytes 524288 | tf_op jit(solution)/shard_map/all_to_all | solution.py:107
  297.7 43.0 %all-to-all-start.3 = ((f32[64,24,256]{2,1,0:T(8,128)}), f32[64,24,256]{2,1,0:T(8,128)S(1)}, u32[]{:S(2)}, u32[]{:S(2)}) async-start(f32[64,24,256]{2,1,0:T(8,128)} %fusion.19), calls=%async_computation.3 | async-start | bytes 3145728 | tf_op jit(solution)/shard_map/all_to_all | solution.py:113
  302.4 287.7 %all-reduce.2.cloned.1.call-start = ((), (), s32[]{:S(2)}) async-start(), calls=%async_computation.4 | async-start | bytes 794624 | tf_op jit(solution)/shard_map/psum | solution.py:119
Sparse Core Ops, SparseCore 0:
  342.3 247.6 all-reduce.1
where the time goes:
time: 601 us; the launch traced here: 600 us
  waiting for transfers between devices  287 us (48%)
  blocking collectives  169 us (28%)
  starting transfers between devices  58.5 us (10%)
  matrix products  29.6 us (5%)
  local copies, waits for them, and re-layouts  25.5 us (4%)
  other arithmetic  15.3 us (3%)
  between operations  14.4 us (2%)
    psum x1, waiting for transfers between devices, together(): total = lax.psum(ravelled, axis)  247 us
    all_gather x1, blocking collectives, in_one_piece(): filled, at, done = (lax.all_gather(both, axis, axis=dim, tiled=True), 0, [])  136 us
    all_to_all x2, starting transfers between devices, sent_to_all(): return lax.all_to_all(copies, axis, split_axis=0, concat_axis=0, tiled=True)  39.4 us
    all_to_all x1, waiting for transfers between devices, sent_and_summed_2(): lax.all_to_all(parts, axis, split_axis=0, concat_axis=0, tiled=True)  37.4 us
    all_gather x3, blocking collectives, collected_together_2(): both, at, found = (lax.all_gather(jnp.concatenate(lines), axis), 0, {})  32.7 us
    all_to_all x1, starting transfers between devices, sent_and_summed(): parts = lax.all_to_all(cut_along(shard, dim, size), axis, 0, 0, tiled=True)  14.4 us
  transfers between devices with their start and end apart: 5, of which 3 were waited for; matrix products, arithmetic and copies ran while one was open for 7% of the time, Pallas kernels for 0%

commit v1 on v0

--- a/solution.py
+++ b/solution.py
@@ -116,7 +116,10 @@
 
 def together(arrays, axis):
     ravelled, at, done = (jnp.concatenate([a.reshape(-1) for a in arrays]), 0, [])
-    total = lax.psum(ravelled, axis)
+    begin_sources_all = lambda target, axis_name: jnp.sum(
+        jax.lax.all_gather(target, axis_name), axis=0
+    )
+    total = begin_sources_all(ravelled, axis)
     for a in arrays:
         done.append(total[at : at + a.size].reshape(a.shape))
         at += a.size

time: 601 us -> 943 us (1.57)
  waiting for transfers between devices: 287 us -> 541 us
  other arithmetic: 15.3 us -> 93 us
  blocking collectives: 169 us -> 183 us
    all_gather x0 -> x1, waiting for transfers between devices: none -> 518 us  [together(): jax.lax.all_gather(target, axis_name)]
    psum x1 -> x0, waiting for transfers between devices: 247 us -> none  [together(): total = lax.psum(ravelled, axis)]
    reduce_sum x0 -> x1, other arithmetic: none -> 78.6 us  [together(): jnp.sum(jax.lax.all_gather(target, axis_name), axis=0)]
    all_to_all x1 -> x0, starting transfers between devices: 14.4 us -> none  [sent_and_summed(): parts = lax.all_to_all(cut_along(shard, dim, size), axis, 0, 0, tiled=True)]
    all_to_all x0 -> x1, blocking collectives: none -> 14.3 us  [sent_and_summed(): parts = lax.all_to_all(cut_along(shard, dim, size), axis, 0, 0, tiled=True)]
    all_to_all x1, waiting for transfers between devices: 37.4 us -> 23.6 us  [sent_and_summed_2(): lax.all_to_all(parts, axis, split_axis=0, concat_axis=0, tiled=True)]
    all_to_all x2, starting transfers between devices: 39.4 us -> 52.7 us  [sent_to_all(): return lax.all_to_all(copies, axis, split_axis=0, concat_axis=0, tiled=True)]
  transfers between devices with their start and end apart: 5 -> 4, of which waited for: 3 -> 3; matrix products, arithmetic and copies ran while one was open for 7% -> 3% of each run, Pallas kernels for 0% -> 0%
where the time goes in v1:
time: 943 us; the launch traced here: 940 us
  waiting for transfers between devices  541 us (57%)
  blocking collectives  183 us (19%)
  other arithmetic  93 us (10%)
  starting transfers between devices  57.6 us (6%)
  matrix products  26.5 us (3%)
  local copies, waits for them, and re-layouts  24.8 us (3%)
  between operations  14.4 us (2%)
    all_gather x1, waiting for transfers between devices, together(): jax.lax.all_gather(target, axis_name)  518 us
    all_gather x1, blocking collectives, in_one_piece(): filled, at, done = (lax.all_gather(both, axis, axis=dim, tiled=True), 0, [])  136 us
    reduce_sum x1, other arithmetic, together(): jnp.sum(jax.lax.all_gather(target, axis_name), axis=0)  78.6 us
    all_to_all x2, starting transfers between devices, sent_to_all(): return lax.all_to_all(copies, axis, split_axis=0, concat_axis=0, tiled=True)  52.7 us
    all_gather x3, blocking collectives, collected_together_2(): both, at, found = (lax.all_gather(jnp.concatenate(lines), axis), 0, {})  32.1 us
    all_to_all x1, waiting for transfers between devices, sent_and_summed_2(): lax.all_to_all(parts, axis, split_axis=0, concat_axis=0, tiled=True)  23.6 us
  transfers between devices with their start and end apart: 4, of which 3 were waited for; matrix products, arithmetic and copies ran while one was open for 3% of the time, Pallas kernels for 0%

profile of v1, /device:TPU:1, one launch (start us, length us, event | category | flops | bytes accessed | tf_op | source)
XLA Modules:
  0.0 940.4 jit_solution(12281712484947794744)
XLA Ops:
  7.2 0.0 copy-start
  7.2 1.0 convert_reduce_fusion.1
  8.2 1.0 fusion.23
  9.2 1.0 fusion.25
  10.2 0.7 broadcast_in_dim.27
  10.9 6.6 all-to-all-start
  17.5 0.7 convert_bitcast_fusion
  18.1 0.8 convert_reduce_fusion.2
  19.0 0.9 fusion.31
  19.9 0.1 copy.35
  20.0 0.8 fusion.33
  20.8 136.4 %all_gather.27 = bf16[1536,257]{1,0:T(8,128)(2,1)S(1)} all-gather(bf16[24,257]{1,0:T(8,128)(2,1)S(1)} %pad_maximum_fusion.4), channel_id=1, replica_groups=mesh['img_0'=4,'img_1'=8,'img_2'=2,'txt'=4] {'img_0','img_1','img_2'}, dimensions={0}, use_global_device_ids=true | all-gather | bytes 801840 | tf_op jit(solution)/shard_map/all_gather | solution.py:35
  157.2 3.0 convolution_convert_fusion
  160.2 0.0 copy-start.3
  160.2 0.0 copy-start.4
  160.3 3.5 fusion.94
  163.8 0.3 compare_reduce_fusion
  164.1 0.0 all-to-all-done
  164.1 0.0 copy-done.3
  164.1 0.0 copy-done.4
  164.1 0.7 convolution_convert_fusion.1
  164.8 1.2 fusion.95
  166.0 0.5 copy.42
  166.5 4.7 multiply_reduce_fusion
  171.2 5.3 exponential_reduce_fusion
  176.5 9.2 all-gather
  185.8 0.1 fusion.60
  185.9 18.9 %all-gather.1 = f32[64,1536]{1,0:T(8,128)S(1)} all-gather(f32[8,1536]{1,0:T(8,128)S(1)} %pad_maximum_fusion.2), channel_id=3, replica_groups=mesh['img_0'=4,'img_1'=8,'img_2'=2,'txt'=4] {'img_1'}, dimensions={0}, use_global_device_ids=true | all-gather | bytes 442368 | tf_op jit(solution)/shard_map/all_gather | solution.py:81
  204.8 0.1 fusion.39
  205.0 3.9 all-gather.2
  208.9 4.2 fusion.1
  213.1 5.9 copy.40
  219.0 6.1 convert_element_type.72
  225.1 4.1 fusion.19
  229.2 4.9 all-to-all-start.3
  234.1 0.0 all-gather.7.cloned.1.call-start
  234.1 0.1 convert_reduce_fusion.3
  234.2 23.6 %all-to-all-done.3 = f32[64,24,256]{2,1,0:T(8,128)S(1)} async-done(((f32[64,24,256]{2,1,0:T(8,128)}), f32[64,24,256]{2,1,0:T(8,128)S(1)}, u32[]{:S(2)}, u32[]{:S(2)}) %all-to-all-start.3) | async-done | bytes 1572896 | tf_op jit(solution)/shard_map/all_to_all | solution.py:113
  257.8 0.1 reduce_sum.97
  258.0 0.0 copy-done.5
  258.0 0.0 copy-done.6
  258.0 0.3 convolution_bitcast_fusion
  258.3 0.2 copy.45
  258.6 1.0 reshape.123
  259.6 0.0 all-gather.7.cloned.1.call-update
  259.6 0.6 broadcast_in_dim.50
  260.3 46.1 %all-to-all-start.1 = ((f32[4,8,512]{2,1,0:T(8,128)}), f32[4,8,512]{2,1,0:T(8,128)S(1)}, u32[]{:S(2)}, u32[]{:S(2)}) async-start(f32[4,8,512]{2,1,0:T(8,128)} %broadcast_in_dim.50), calls=%async_computation.1 | async-start | bytes 131072 | tf_op jit(solution)/shard_map/all_to_all | solution.py:18
  306.4 4.7 copy.41
  311.0 0.1 all-to-all-done.1
  311.2 0.0 copy-start.9
  311.2 0.0 copy-start.2
  311.2 0.0 copy-start.8
  311.2 9.0 fusion.9
  320.3 0.0 copy-done.9
  320.3 0.5 convolution_convert_fusion.2
  320.8 14.3 %all_to_all.20 = bf16[4,128,256]{2,1,0:T(8,128)(2,1)S(1)} all-to-all(bf16[4,128,256]{2,1,0:T(8,128)(2,1)S(1)} %bitcast.315), channel_id=1, replica_groups=mesh['img_0'=4,'img_1'=8,'img_2'=2,'txt'=4] {'txt'}, dimensions={0} | all-to-all | bytes 524288 | tf_op jit(solution)/shard_map/all_to_all | solution.py:107
  335.1 0.0 copy-done.2
  335.2 0.0 copy-done.8
  335.2 0.7 fusion.26
  335.8 0.6 fusion.81
  336.4 517.5 %all-gather.7.cloned.1.call-done = f32[256,1,98688]{2,1,0:T(1,128)} async-done(((f32[1,1,98688]{2,1,0:T(1,128)}), f32[256,1,98688]{2,1,0:T(1,128)}) %all-gather.7.cloned.1.call-update) | async-done | bytes 101056528 | tf_op jit(solution)/shard_map/all_gather | solution.py:120
  853.9 78.6 %reduce_sum.99 = f32[98688]{0:T(1024)S(1)} reduce(f32[256,1,98688]{2,1,0:T(1,128)} %all-gather.7.cloned.1.call-done, f32[]{:T(128)} %constant.8.clone.1), dimensions={0,1}, to_apply=%region_11.12 | reduce | flops 25165440 | bytes 101451264 | tf_op jit(solution)/shard_map/reduce_sum | solution.py:119
  932.5 0.1 reshape.118
  932.6 0.9 broadcast_divide_fusion
  (27 shorter events, 0.3 us)
Async XLA Ops:
  7.2 218.0 %copy-start = (bf16[1024,256]{1,0:T(8,128)(2,1)S(1)}, bf16[1024,256]{1,0:T(8,128)(2,1)}, u32[]{:S(2)}) copy-start(bf16[1024,256]{1,0:T(8,128)(2,1)} %param.25) | copy-start | bytes 1572868
  10.9 153.1 %all-to-all-start = ((bf16[4,128,256]{2,1,0:T(8,128)(2,1)}), bf16[4,128,256]{2,1,0:T(8,128)(2,1)S(1)}, u32[]{:S(2)}, u32[]{:S(2)}) async-start(bf16[4,128,256]{2,1,0:T(8,128)(2,1)} %broadcast_in_dim.27), calls=%async_computation | async-start | bytes 524288 | tf_op jit(solution)/shard_map/all_to_all | solution.py:18
  160.2 3.8 copy-start.3
  160.2 3.8 copy-start.4
  171.2 37.7 %copy-start.1 = (f32[4,512,1536]{2,1,0:T(8,128)}, f32[4,512,1536]{2,1,0:T(8,128)S(1)}, u32[]{:S(2)}) copy-start(f32[4,512,1536]{2,1,0:T(8,128)S(1)} %get-tuple-element.23) | copy-start | bytes 37748740
  219.0 15.1 %copy-start.10 = (s32[24]{0:T(128)S(1)}, s32[24]{0:T(128)}, u32[]{:S(2)}) copy-start(s32[24]{0:T(128)} %param.17) | copy-start | bytes 292
  219.0 15.1 %copy-start.7 = (s32[24]{0:T(128)S(1)}, s32[24]{0:T(128)}, u32[]{:S(2)}) copy-start(s32[24]{0:T(128)} %param.16) | copy-start | bytes 292
  225.1 32.8 %copy-start.5 = (bf16[24,256]{1,0:T(8,128)(2,1)S(1)}, bf16[24,256]{1,0:T(8,128)(2,1)}, u32[]{:S(2)}) copy-start(bf16[24,256]{1,0:T(8,128)(2,1)} %param.15) | copy-start | bytes 36868
  225.1 32.8 %copy-start.6 = (f32[256]{0:T(256)S(1)}, f32[256]{0:T(256)}, u32[]{:S(2)}) copy-start(f32[256]{0:T(256)} %param.27) | copy-start | bytes 3076
  229.2 28.6 %all-to-all-start.3 = ((f32[64,24,256]{2,1,0:T(8,128)}), f32[64,24,256]{2,1,0:T(8,128)S(1)}, u32[]{:S(2)}, u32[]{:S(2)}) async-start(f32[64,24,256]{2,1,0:T(8,128)} %fusion.19), calls=%async_computation.3 | async-start | bytes 3145728 | tf_op jit(solution)/shard_map/all_to_all | solution.py:113
  234.1 619.9 %all-gather.7.cloned.1.call-start = ((), (), s32[]{:S(2)}) async-start(), calls=%async_computation.4 | async-start | bytes 101451264 | tf_op jit(solution)/shard_map/all_gather | solution.py:120
  260.3 50.9 %all-to-all-start.1 = ((f32[4,8,512]{2,1,0:T(8,128)}), f32[4,8,512]{2,1,0:T(8,128)S(1)}, u32[]{:S(2)}, u32[]{:S(2)}) async-start(f32[4,8,512]{2,1,0:T(8,128)} %broadcast_in_dim.50), calls=%async_computation.1 | async-start | bytes 131072 | tf_op jit(solution)/shard_map/all_to_all | solution.py:18
  311.2 9.1 copy-start.9
  311.2 23.9 %copy-start.2 = (bf16[128,256]{1,0:T(8,128)(2,1)S(1)}, bf16[128,256]{1,0:T(8,128)(2,1)}, u32[]{:S(2)}) copy-start(bf16[128,256]{1,0:T(8,128)(2,1)} %param.14) | copy-start | bytes 196612
  311.2 23.9 %copy-start.8 = (f32[256]{0:T(256)S(1)}, f32[256]{0:T(256)}, u32[]{:S(2)}) copy-start(f32[256]{0:T(256)} %param.26) | copy-start | bytes 3076
Sparse Core Ops, SparseCore 0:
  259.7 594.1 all-gather.6
